TPU v7x, 32 devices: a whole 2x2x4 slice. The times are simulated.
32 devices in a mesh: row: 4 (over y, x), col: 8 (over z, core).
Axes of the slice: x: 2, y: 2, z: 4, core: 2. Of those that a mesh axis runs over, the one named last changes fastest.
Arguments:
- activations: bfloat16 [256, 16384], P(None, 'row'), may hold values from -3 to 3
- cotangent: bfloat16 [256, 16384], P(None, 'row'), may hold values from -0.59765625 to 0.59765625
- forget: int32 [256], replicated, may hold values 0 or 1
- lengths: int32 [4, 4], P('row'), may hold values from 1 to 32, 64 in all within a row
- query_weight: bfloat16 [16384, 8192], P('row', 'col'), may hold values from -0.046875 to 0.046875
- key_weight: bfloat16 [16384, 512], P('row'), may hold values from -0.046875 to 0.046875
- value_weight: bfloat16 [16384, 512], P('row'), may hold values from -0.046875 to 0.046875
- output_projection_weight: bfloat16 [8192, 16384], P('col', 'row'), may hold values from -0.0625 to 0.0625
- query_down: bfloat16 [16384, 32], P('row'), may hold values from -0.046875 to 0.046875
- query_up: bfloat16 [32, 8192], P(None, 'col'), may hold values from -1 to 1
- output_down: bfloat16 [8192, 32], P('col'), may hold values from -0.0625 to 0.0625
- output_up: bfloat16 [32, 16384], P(None, 'row'), may hold values from -1 to 1
Outputs:
- query_down_gradient: float32 [16384, 32], P('row')
- query_up_gradient: float32 [32, 8192], P(None, 'col')
- output_down_gradient: float32 [8192, 32], P('col')
- output_up_gradient: float32 [32, 16384], P(None, 'row')
Inputs may be any that keep to these rules, and one draw needn't show every extreme that they name: In every row of lengths the 4 values sum to 64, and the largest is exactly 32.
All inputs are finite; a program needn't handle non-finite values.
Results may differ from a plain program's by a relative error of at most 0.025.
Values may be sent and summed in bfloat16 or wider, within the bound.
A program may use at most 128 MiB of HBM per device.

v0:
```python
import math

import jax
import jax.numpy as jnp
from jax import lax
from jax.sharding import PartitionSpec as P

HD = 128
HEADS = 64
KVH = 4


adapter_scale = 0.5
highest_precision = lax.Precision.HIGHEST


def row_contraction(left, right):
    return lax.dot_general(
        left, right, (((1,), (1,)), ((), ())), preferred_element_type=jnp.float32
    )


def token_contraction(left, right):
    return lax.dot_general(
        left, right, (((0,), (0,)), ((), ())), preferred_element_type=jnp.float32
    )


def local(
    activations,
    cotangent,
    forget,
    lengths,
    query_weight,
    key_weight,
    value_weight,
    output_projection_weight,
    query_down,
    query_up,
    output_down,
    output_up,
):
    row_index = lax.axis_index("row")
    col_index = lax.axis_index("col")
    tok_blk = activations.shape[0] // lax.axis_size("row")
    query_cols = query_weight.shape[1]
    heads_dev = query_cols // HD
    group_index = col_index * heads_dev // (HEADS // KVH)
    inverse = 1.0 / math.sqrt(HD)
    up_projection_broad = query_up.astype(jnp.float32)
    down_projection_broad = output_down.astype(jnp.float32)
    key_slice = lax.dynamic_slice_in_dim(key_weight, group_index * HD, HD, 1)
    value_slice = lax.dynamic_slice_in_dim(value_weight, group_index * HD, HD, 1)
    kv_cols = key_slice.shape[1]
    block_of_rows = activations
    reduced_result = jnp.dot(block_of_rows, query_down, preferred_element_type=jnp.float32)
    query_partial_term = jnp.dot(block_of_rows, query_weight, preferred_element_type=jnp.float32)
    query_partial_term = query_partial_term + adapter_scale * jnp.dot(
        reduced_result, up_projection_broad, precision=highest_precision
    )
    key_term = jnp.dot(block_of_rows, key_slice, preferred_element_type=jnp.float32)
    value_term = jnp.dot(block_of_rows, value_slice, preferred_element_type=jnp.float32)
    summed = lax.psum_scatter(
        jnp.concatenate([query_partial_term, key_term, value_term, reduced_result], axis=1).astype(
            jnp.bfloat16
        ),
        "row",
        scatter_dimension=0,
        tiled=True,
    ).astype(jnp.float32)
    query_heads = summed[:, :query_cols].astype(jnp.bfloat16).reshape(tok_blk, heads_dev, HD)
    key_part = summed[:, query_cols : query_cols + kv_cols].astype(jnp.bfloat16)
    value_part = summed[:, query_cols + kv_cols : query_cols + 2 * kv_cols].astype(jnp.bfloat16)
    input_lowrank_factor = summed[:, query_cols + 2 * kv_cols :]
    seg_ends = jnp.cumsum(lengths[0])
    position = jnp.arange(tok_blk, dtype=jnp.int32)
    segment = jnp.sum((position[:, None] >= seg_ends[None, :]).astype(jnp.int32), axis=1)
    allowed = (segment[:, None] == segment[None, :]) & (position[None, :] <= position[:, None])
    scores = (
        jnp.einsum("qhd,kd->hqk", query_heads, key_part, preferred_element_type=jnp.float32)
        * inverse
    )
    numerator = jnp.where(allowed[None], jnp.exp(scores), 0.0)
    softmax = numerator / jnp.sum(numerator, axis=2, keepdims=True)
    weights = softmax.astype(jnp.bfloat16)
    hidden_state = jnp.einsum(
        "hqk,kd->qhd", weights, value_part, preferred_element_type=jnp.float32
    )
    hidden_state = hidden_state.reshape(tok_blk, query_cols).astype(jnp.bfloat16)
    sign_flip = (1 - 2 * forget).astype(jnp.bfloat16)
    output_gradient = cotangent * sign_flip[:, None]
    block_of_rows = output_gradient
    reduced_result = row_contraction(block_of_rows, output_up)
    hidden_state_term = row_contraction(
        block_of_rows, output_projection_weight
    ) + adapter_scale * jnp.dot(
        reduced_result, down_projection_broad.T, precision=highest_precision
    )
    backward = lax.psum_scatter(
        jnp.concatenate([hidden_state_term, reduced_result], axis=1).astype(jnp.bfloat16),
        "row",
        scatter_dimension=0,
        tiled=True,
    ).astype(jnp.float32)
    hidden_grad = backward[:, :query_cols].astype(jnp.bfloat16).reshape(tok_blk, heads_dev, HD)
    gradient_lowrank_factor = backward[:, query_cols:]
    prob_grad = jnp.einsum(
        "qhd,kd->hqk", hidden_grad, value_part, preferred_element_type=jnp.float32
    )
    score_grad = softmax * (prob_grad - jnp.sum(prob_grad * softmax, axis=2, keepdims=True))
    query_gradient = (
        jnp.einsum(
            "hqk,kd->qhd", score_grad, key_part.astype(jnp.float32), precision=highest_precision
        )
        * inverse
    )
    query_gradient = query_gradient.reshape(tok_blk, query_cols)
    query_lowrank_factor = jnp.dot(
        query_gradient, up_projection_broad.T, precision=highest_precision
    )
    hidden_state_factor = jnp.dot(hidden_state, output_down, preferred_element_type=jnp.float32)
    up_projection_piece = adapter_scale * jnp.dot(
        input_lowrank_factor.T, query_gradient, precision=highest_precision
    )
    down_projection_piece = adapter_scale * jnp.dot(
        hidden_state.astype(jnp.float32).T, gradient_lowrank_factor, precision=highest_precision
    )
    query_up_gradient, output_down_gradient = (
        lax.psum(up_projection_piece.astype(jnp.bfloat16), "row").astype(jnp.float32),
        lax.psum(down_projection_piece.astype(jnp.bfloat16), "row").astype(jnp.float32),
    )
    zero_rows = jnp.zeros((activations.shape[0], query_lowrank_factor.shape[1]), jnp.float32)
    first_token = row_index * tok_blk
    query_padded = lax.dynamic_update_slice_in_dim(zero_rows, query_lowrank_factor, first_token, 0)
    hidden_padded = lax.dynamic_update_slice_in_dim(zero_rows, hidden_state_factor, first_token, 0)
    query_total, hidden_total = lax.psum((query_padded, hidden_padded), ("row", "col"))
    query_everywhere = query_total.astype(jnp.bfloat16)
    hidden_state_everywhere = hidden_total.astype(jnp.bfloat16)
    query_down_gradient = adapter_scale * token_contraction(activations, query_everywhere)
    output_up_gradient = adapter_scale * token_contraction(hidden_state_everywhere, output_gradient)
    return (query_down_gradient, query_up_gradient, output_down_gradient, output_up_gradient)


def solution(mesh):
    placed = (
        P(None, "row"),
        P(None, "row"),
        P(),
        P("row", None),
        P("row", "col"),
        P("row", None),
        P("row", None),
        P("col", "row"),
        P("row", None),
        P(None, "col"),
        P("col", None),
        P(None, "row"),
    )
    return jax.shard_map(
        local,
        mesh=mesh,
        in_specs=placed,
        out_specs=(P("row", None), P(None, "col"), P("col", None), P(None, "row")),
        check_vma=False,
    )
```

profile of v0, /device:TPU:0, one launch (start us, length us, event | category | flops | bytes accessed | tf_op | source)
XLA Modules:
  0.0 180.6 jit_solution(12886477900674417634)
XLA Ops:
  7.2 0.0 copy-start
  7.2 0.0 reduce-scatter.3.cloned.1.call-start
  7.2 1.5 copy-done
  8.8 1.7 fusion.58
  10.5 0.1 copy.46
  10.6 1.9 %fusion.17 = bf16[256,128]{1,0:T(8,128)(2,1)S(1)} fusion(bf16[256,4096]{1,0:T(8,128)(2,1)S(1)} %copy-done, bf16[4096,512]{1,0:T(8,128)(2,1)} %param.17, s32[]{:T(128)S(6)} %select_n.18), kind=kOutput, calls=%fused_computation.29 | convolution fusion | flops 268468224 | bytes 3211268 | tf_op jit(solution)/shard_map/dot_general | solution.py:61
  12.5 1.9 %fusion.18 = bf16[256,128]{1,0:T(8,128)(2,1)S(1)} fusion(bf16[256,4096]{1,0:T(8,128)(2,1)S(1)} %copy-done, bf16[4096,512]{1,0:T(8,128)(2,1)} %param.18, s32[]{:T(128)S(6)} %select_n.18), kind=kOutput, calls=%fused_computation.30 | convolution fusion | flops 268468224 | bytes 3211268 | tf_op jit(solution)/shard_map/dot_general | solution.py:62
  14.4 0.0 copy-start.1
  14.4 5.7 %fusion.60 = f32[256,1024]{1,0:T(8,128)S(1)} fusion(bf16[256,4096]{1,0:T(8,128)(2,1)S(1)} %copy-done, bf16[4096,1024]{1,0:T(8,128)(2,1)} %param.16), kind=kOutput, calls=%fused_computation.79 | convolution fusion | flops 2147483648 | bytes 11534336 | tf_op jit(solution)/shard_map/dot_general | solution.py:57
  20.2 0.0 copy-start.4
  20.2 0.0 copy-start.3
  20.2 0.0 copy-done.1
  20.2 0.7 fusion.8
  20.9 0.9 pad_maximum_fusion
  21.8 0.0 reduce-scatter.3.cloned.1.call-update
  21.8 0.0 reduce-scatter.5.cloned.1.call-start
  21.9 0.0 copy-done.4
  21.9 0.0 copy-done.3
  21.9 2.4 %fusion.59 = (bf16[256,32]{0,1:T(8,128)(2,1)S(1)}, f32[256,32]{0,1:T(8,128)S(1)}) fusion(bf16[32,4096]{1,0:T(8,128)(2,1)S(1)} %copy-done.3, bf16[256,4096]{1,0:T(8,128)(2,1)} %param.13, bf16[256]{0:T(256)(128)(2,1)S(1)} %subtract_convert_fusion), kind=kOutput, calls=%fused_computation.78 | convolution fusion | flops 68165632 | bytes 2408960 | tf_op jit(solution)/shard_map/dot_general | solution.py:18
  24.3 0.1 copy.48
  24.5 0.0 copy-start.2
  24.5 6.4 %fusion.4 = f32[256,1024]{1,0:T(8,128)S(1)} fusion(bf16[1024,4096]{1,0:T(8,128)(2,1)} %param.19, bf16[256,4096]{1,0:T(8,128)(2,1)} %param.13, bf16[256]{0:T(256)(128)(2,1)S(1)} %subtract_convert_fusion), kind=kOutput, calls=%fused_computation.6 | convolution fusion | flops 2148532224 | bytes 11534848 | tf_op jit(solution)/shard_map/dot_general | solution.py:18
  30.9 0.0 copy-start.5
  30.9 0.0 copy-done.2
  30.9 0.6 fusion.9
  31.5 0.9 pad_maximum_fusion.1
  32.4 0.0 reduce-scatter.5.cloned.1.call-update
  32.4 0.0 all-reduce.4.cloned.1.call-start
  32.5 0.0 copy-done.5
  32.5 0.2 reduce-window.8
  32.7 0.1 convert_reduce_fusion
  32.8 0.1 fusion.44
  32.8 17.6 %reduce-scatter.3.cloned.1.call-done = bf16[64,1312]{1,0:T(8,128)(2,1)} async-done(((bf16[256,1312]{1,0:T(8,128)(2,1)}), bf16[64,1312]{1,0:T(8,128)(2,1)}) %reduce-scatter.3.cloned.1.call-update) | async-done | bytes 167952 | tf_op jit(solution)/shard_map/reduce_scatter | solution.py:63
  50.4 1.2 fusion.41
  51.7 0.9 fusion.14
  52.6 0.1 fusion.31
  52.7 25.9 %reduce-scatter.5.cloned.1.call-done = bf16[64,1056]{1,0:T(8,128)(2,1)} async-done(((bf16[256,1056]{1,0:T(8,128)(2,1)}), bf16[64,1056]{1,0:T(8,128)(2,1)}) %reduce-scatter.5.cloned.1.call-update) | async-done | bytes 135184 | tf_op jit(solution)/shard_map/reduce_scatter | solution.py:99
  78.7 1.2 multiply_reduce_fusion
  79.8 1.1 fusion.10
  81.0 0.3 fusion.25
  81.2 0.3 dynamic_update_slice.7
  81.6 0.3 dynamic_update_slice.6
  82.0 39.9 %all-reduce = (bf16[256,32]{0,1:T(8,128)(2,1)S(1)}, bf16[256,32]{0,1:T(8,128)(2,1)S(1)}) all-reduce(f32[256,32]{0,1:T(8,128)S(1)} %dynamic_update_slice.6, f32[256,32]{0,1:T(8,128)S(1)} %dynamic_update_slice.7), channel_id=1, replica_groups=mesh['row'=4,'col'=8] {'row','col'}, use_global_device_ids=true, to_apply=%region_6.7 | all-reduce | flops 16384 | bytes 98304 | tf_op jit(solution)/shard_map/psum | solution.py:136
  121.9 2.9 %convolution_multiply_fusion = f32[32,4096]{1,0:T(8,128)} fusion(bf16[256,4096]{1,0:T(8,128)(2,1)} %param.13, bf16[256]{0:T(256)(128)(2,1)S(1)} %subtract_convert_fusion, bf16[256,32]{0,1:T(8,128)(2,1)S(1)} %get-tuple-element.5), kind=kOutput, calls=%fused_computation | convolution fusion | flops 68288512 | bytes 2638336 | tf_op jit(solution)/shard_map/dot_general | solution.py:24
  124.8 1.6 fusion.16
  126.4 1.6 fusion.15
  128.0 0.0 all-reduce.4.cloned.1.call-update
  128.0 1.3 fusion
  129.2 41.8 %all-reduce.4.cloned.1.call-done = (bf16[32,1024]{1,0:T(8,128)(2,1)}, bf16[1024,32]{0,1:T(8,128)(2,1)}) async-done(((bf16[32,1024]{1,0:T(8,128)(2,1)}, bf16[1024,32]{0,1:T(8,128)(2,1)}), (bf16[32,1024]{1,0:T(8,128)(2,1)}, bf16[1024,32]{0,1:T(8,128)(2,1)})) %all-reduce.4.cloned.1.call-update) | async-done | bytes 131088 | tf_op jit(solution)/shard_map/psum | solution.py:129
  171.0 1.5 convert_element_type.52
  172.5 1.5 convert_element_type.58
  (3 shorter events, 0.0 us)
Async XLA Ops:
  7.2 1.6 copy-start
  7.2 43.3 %reduce-scatter.3.cloned.1.call-start = ((), (), s32[]{:S(2)}) async-start(), calls=%async_computation.2 | async-start | bytes 901120 | tf_op jit(solution)/shard_map/reduce_scatter | solution.py:63
  14.4 5.8 %copy-start.1 = (bf16[32,1024]{1,0:T(8,128)(2,1)S(1)}, bf16[32,1024]{1,0:T(8,128)(2,1)}, u32[]{:S(2)}) copy-start(bf16[32,1024]{1,0:T(8,128)(2,1)} %param.21) | copy-start | bytes 196612
  20.2 1.7 copy-start.4
  20.2 1.7 copy-start.3
  21.8 56.8 %reduce-scatter.5.cloned.1.call-start = ((), (), s32[]{:S(2)}) async-start(), calls=%async_computation.3 | async-start | bytes 737280 | tf_op jit(solution)/shard_map/reduce_scatter | solution.py:99
  24.5 6.4 %copy-start.2 = (bf16[1024,32]{0,1:T(8,128)(2,1)S(1)}, bf16[1024,32]{0,1:T(8,128)(2,1)}, u32[]{:S(2)}) copy-start(bf16[1024,32]{0,1:T(8,128)(2,1)} %param.22) | copy-start | bytes 196612
  30.9 1.6 copy-start.5
  32.4 138.6 %all-reduce.4.cloned.1.call-start = ((), (), s32[]{:S(2)}) async-start(), calls=%async_computation.4 | async-start | bytes 262144 | tf_op jit(solution)/shard_map/psum | solution.py:129
Sparse Core Ops, SparseCore 0:
  22.0 28.4 reduce-scatter.2
  53.6 25.0 reduce-scatter.4
  128.1 42.8 all-reduce.3
where the time goes:
time: 181 us
  waiting for transfers between devices  85.3 us (47%)
  blocking collectives  39.9 us (22%)
  matrix products  33.5 us (19%)
  between operations  14 us (8%)
  other arithmetic  5.14 us (3%)
  local copies, waits for them, and re-layouts  2.51 us (1%)
    psum x1, waiting for transfers between devices, local(): lax.psum(up_projection_piece.astype(jnp.bfloat16), 'row')  41.8 us
    psum x1, blocking collectives, local(): lax.psum((query_padded, hidden_padded), ('row', 'col'))  39.9 us
    reduce_scatter x1, waiting for transfers between devices, local(): lax.psum_scatter(jnp.concatenate([hidden_state_term, reduced_result], axi...  25.9 us
    reduce_scatter x1, waiting for transfers between devices, local(): lax.psum_scatter(jnp.concatenate([query_partial_term, key_term, value_ter...  17.6 us
    dot_general x2, matrix products, row_contraction(): lax.dot_general(left, right, (((1,), (1,)), ((), ())), preferred_element_...  8.79 us
    dot_general x1, matrix products, local(): jnp.dot(block_of_rows, query_weight, preferred_element_type=jnp.float32)  5.74 us
    dot_general x2, matrix products, token_contraction(): lax.dot_general(left, right, (((0,), (0,)), ((), ())), preferred_element_...  4.2 us
  transfers between devices with their start and end apart: 3, of which 3 were waited for; matrix products, arithmetic and copies ran while one was open for 8% of the time, Pallas kernels for 0%

commit v1 on v0

v1 whole, which is shorter than its diff:
```python
import functools
import math

import jax
import jax.numpy as jnp
from jax import lax
from jax.experimental import pallas as pl
from jax.experimental.pallas import tpu as pltpu
from jax.sharding import PartitionSpec as P

HD = 128
HEADS = 64
KVH = 4

SCALE = 0.5
BF = jnp.bfloat16
F32 = jnp.float32


def mm(left, right, a, b):
    return lax.dot_general(
        left, right, (((a,), (b,)), ((), ())), preferred_element_type=F32
    )


def kernel(
    n_row,
    n_col,
    lengths_ref,
    forget_ref,
    x_hbm,
    cot_hbm,
    wq_hbm,
    wk_hbm,
    wv_hbm,
    wo_hbm,
    qd_hbm,
    up_hbm,
    od_hbm,
    ou_hbm,
    dq_ref,
    pieces_ref,
    du_ref,
    x,
    cot,
    wq,
    wkv,
    wo,
    qd,
    up,
    od,
    ou,
    red,
    chunk_send,
    chunk_recv,
    small_send,
    small_recv,
    fac_send,
    fac_recv,
    fac_all,
    piece_send,
    piece_recv,
    piece_all,
    load_sem,
    wq_sem,
    wo_sem,
    chunk_ss,
    chunk_rs,
    small_ss,
    small_rs,
    fac_ss,
    fac_rs,
    all_ss,
    all_rs,
    piece_ss,
    piece_rs,
    gat_ss,
    gat_rs,
):
    me = lax.axis_index("row")
    mc = lax.axis_index("col")
    n_chunk, depth, width = wq.shape
    rank = qd.shape[1]
    tokens = x.shape[0]
    blk = tokens // n_row
    heads = n_chunk * width // HD
    per = width // HD
    inverse = 1.0 / math.sqrt(HD)
    group = lax.div(mc * heads, HEADS // KVH)
    group_cols = pl.ds(pl.multiple_of(group * HD, HD), HD)

    def row_peer(d):
        return lax.rem(me + d, n_row)

    def col_peer(d):
        return lax.rem(mc + d, n_col)

    def load_wq(c):
        return pltpu.make_async_copy(
            wq_hbm.at[:, pl.ds(c * width, width)], wq.at[c], wq_sem.at[c]
        )

    def load_wo(c):
        return pltpu.make_async_copy(
            wo_hbm.at[pl.ds(c * width, width), :], wo.at[c], wo_sem.at[c]
        )

    def up_load(c):
        return pltpu.make_async_copy(
            up_hbm.at[:, pl.ds(c * width, width)], up.at[c], load_sem.at[7 + c]
        )

    load_x = pltpu.make_async_copy(x_hbm, x, load_sem.at[0])
    load_qd = pltpu.make_async_copy(qd_hbm, qd, load_sem.at[1])
    load_k = pltpu.make_async_copy(wk_hbm.at[:, group_cols], wkv.at[0], load_sem.at[2])
    load_v = pltpu.make_async_copy(wv_hbm.at[:, group_cols], wkv.at[1], load_sem.at[3])
    load_cot = pltpu.make_async_copy(cot_hbm, cot, load_sem.at[4])
    load_ou = pltpu.make_async_copy(ou_hbm, ou, load_sem.at[5])
    load_od = pltpu.make_async_copy(od_hbm, od, load_sem.at[6])
    load_x.start()
    load_qd.start()
    for c in range(n_chunk):
        up_load(c).start()
    for c in range(n_chunk):
        load_wq(c).start()
    load_k.start()
    load_v.start()
    load_cot.start()
    load_ou.start()
    load_od.start()
    for c in range(n_chunk):
        load_wo(c).start()

    barrier = pltpu.get_barrier_semaphore()
    for d in range(1, n_row):
        pl.semaphore_signal(
            barrier, inc=1, device_id={"row": row_peer(d)}, device_id_type=pl.DeviceIdType.MESH
        )
    for d in range(1, n_col):
        pl.semaphore_signal(
            barrier, inc=1, device_id={"col": col_peer(d)}, device_id_type=pl.DeviceIdType.MESH
        )

    def remote(src, dst, send, recv, where):
        return pltpu.make_async_remote_copy(
            src_ref=src,
            dst_ref=dst,
            send_sem=send,
            recv_sem=recv,
            device_id=where,
            device_id_type=pl.DeviceIdType.MESH,
        )

    def chunk_copy(c, d):
        p = row_peer(d)
        return remote(
            chunk_send.at[c, p], chunk_recv.at[c, d], chunk_ss.at[c, d], chunk_rs.at[c, d], {"row": p}
        )

    def small_copy(d):
        p = row_peer(d)
        return remote(small_send.at[p], small_recv.at[d], small_ss.at[d], small_rs.at[d], {"row": p})

    def fac_copy(d):
        return remote(fac_send, fac_recv.at[d], fac_ss.at[d], fac_rs.at[d], {"col": col_peer(d)})

    def all_copy(d):
        return remote(
            fac_all.at[me], fac_all.at[me], all_ss.at[d], all_rs.at[d], {"row": row_peer(d)}
        )

    def all_arrival(d):
        return remote(
            fac_all.at[me], fac_all.at[row_peer(n_row - d)], all_ss.at[d], all_rs.at[d], {"row": row_peer(d)}
        )

    def piece_copy(d):
        p = row_peer(d)
        return remote(piece_send.at[p], piece_recv.at[d], piece_ss.at[d], piece_rs.at[d], {"row": p})

    def gat_copy(d):
        return remote(
            piece_all.at[me], piece_all.at[me], gat_ss.at[d], gat_rs.at[d], {"row": row_peer(d)}
        )

    def gat_arrival(d):
        return remote(
            piece_all.at[me], piece_all.at[row_peer(n_row - d)], gat_ss.at[d], gat_rs.at[d], {"row": row_peer(d)}
        )

    load_x.wait()
    load_qd.wait()
    for c in range(n_chunk):
        up_load(c).wait()
    lowrank = mm(x[...], qd[...], 1, 0)
    red[0] = lowrank.astype(BF)
    pl.semaphore_wait(barrier, n_row + n_col - 2)

    @pl.loop(0, n_chunk)
    def _(c):
        pltpu.make_async_copy(
            wq_hbm.at[:, pl.ds(0, width)], wq.at[c], wq_sem.at[c]
        ).wait()
        term = mm(x[...], wq[c], 1, 0) + SCALE * mm(red[0], up[c], 1, 0)
        chunk_send[c] = term.astype(BF).reshape(n_row, blk, width)
        for d in range(1, n_row):
            chunk_copy(c, d).start()

    load_k.wait()
    load_v.wait()
    small_send[:, :, 0:HD] = mm(x[...], wkv[0], 1, 0).astype(BF).reshape(n_row, blk, HD)
    small_send[:, :, HD : 2 * HD] = mm(x[...], wkv[1], 1, 0).astype(BF).reshape(n_row, blk, HD)
    load_cot.wait()
    load_ou.wait()
    load_od.wait()
    red[1] = mm(cot[...], ou[...], 1, 1).astype(BF)
    small_send[:, :, 2 * HD :] = jnp.concatenate(
        [red[0], red[1], jnp.zeros((tokens, HD - 2 * rank), BF)], axis=1
    ).reshape(n_row, blk, HD)
    for d in range(1, n_row):
        small_copy(d).start()

    @pl.loop(0, n_chunk)
    def _(c):
        pltpu.make_async_copy(
            wo_hbm.at[pl.ds(0, width), :], wo.at[c], wo_sem.at[c]
        ).wait()
        down = od[pl.ds(pl.multiple_of(c * width, width), width), :]
        term = mm(cot[...], wo[c], 1, 1) + SCALE * mm(red[1], down, 1, 1)
        chunk_send[n_chunk + c] = term.astype(BF).reshape(n_row, blk, width)
        for d in range(1, n_row):
            chunk_copy(n_chunk + c, d).start()

    def chunk_sum(c):
        total = chunk_send[c, me].astype(F32)
        for d in range(1, n_row):
            chunk_copy(c, d).wait_recv()
            total = total + chunk_recv[c, d].astype(F32)
        return total

    def sign_of(first):
        lane = lax.broadcasted_iota(jnp.int32, (blk, tokens), 1)
        sub = lax.broadcasted_iota(jnp.int32, (blk, tokens), 0)
        picked = jnp.where(lane == sub + first, forget_ref[...], 0)
        return (1 - 2 * jnp.sum(picked, axis=1, keepdims=True)).astype(F32)

    sign = sign_of(me * blk)

    stacked = []
    for c in range(n_chunk):
        part = chunk_sum(c).astype(BF)
        for h in range(per):
            stacked.append(part[:, h * HD : (h + 1) * HD])
    query = jnp.concatenate(stacked, axis=0)
    small = small_send[me].astype(F32)
    for d in range(1, n_row):
        small_copy(d).wait_recv()
        small = small + small_recv[d].astype(F32)
    key = small[:, 0:HD].astype(BF)
    value = small[:, HD : 2 * HD].astype(BF)
    in_low = small[:, 2 * HD : 2 * HD + rank].astype(BF)
    grad_low = (small[:, 2 * HD + rank : 2 * HD + 2 * rank] * sign).astype(BF)

    rows = heads * blk
    pos_q = lax.rem(lax.broadcasted_iota(jnp.int32, (rows, blk), 0), blk)
    pos_k = lax.broadcasted_iota(jnp.int32, (rows, blk), 1)
    seg_q = jnp.zeros((rows, blk), jnp.int32)
    seg_k = jnp.zeros((rows, blk), jnp.int32)
    end = 0
    for i in range(lengths_ref.shape[1]):
        end = end + lengths_ref[0, i]
        seg_q = seg_q + (pos_q >= end).astype(jnp.int32)
        seg_k = seg_k + (pos_k >= end).astype(jnp.int32)
    allowed = (seg_q == seg_k) & (pos_k <= pos_q)
    scores = mm(query, key, 1, 1) * inverse
    numer = jnp.where(allowed, jnp.exp(scores), 0.0)
    softmax = numer / jnp.sum(numer, axis=1, keepdims=True)
    hidden = mm(softmax.astype(BF), value, 1, 0).astype(BF)
    hidden_flat = jnp.concatenate([hidden[h * blk : (h + 1) * blk] for h in range(heads)], axis=1)
    hidden_factor = mm(hidden_flat, od[...], 1, 0)
    down_piece = SCALE * mm(grad_low, hidden_flat, 0, 0)

    stacked = []
    for c in range(n_chunk):
        part = (chunk_sum(n_chunk + c) * sign).astype(BF)
        for h in range(per):
            stacked.append(part[:, h * HD : (h + 1) * HD])
    hidden_grad = jnp.concatenate(stacked, axis=0)
    prob_grad = mm(hidden_grad, value, 1, 1)
    score_grad = softmax * (prob_grad - jnp.sum(prob_grad * softmax, axis=1, keepdims=True))
    query_grad = (mm(score_grad.astype(BF), key, 1, 0) * inverse).astype(BF)
    grad_flat = jnp.concatenate(
        [query_grad[h * blk : (h + 1) * blk] for h in range(heads)], axis=1
    )
    query_factor = mm(grad_flat[:, 0:width], up[0], 1, 1)
    for c in range(1, n_chunk):
        query_factor = query_factor + mm(grad_flat[:, c * width : (c + 1) * width], up[c], 1, 1)
    factors = jnp.concatenate([query_factor, hidden_factor], axis=1)
    half = blk // 2
    packed = jnp.concatenate([factors[:half], factors[half:]], axis=1)
    fac_send[...] = packed.astype(BF)
    for d in range(1, n_col):
        fac_copy(d).start()
    up_piece = SCALE * mm(in_low, grad_flat, 0, 0)
    both = jnp.concatenate([up_piece, down_piece], axis=0).astype(BF)
    share = piece_send.shape[1]
    for r in range(n_row):
        piece_send[r] = both[r * share : (r + 1) * share]
    for d in range(1, n_row):
        piece_copy(d).start()

    total = fac_send[...].astype(F32)
    for d in range(1, n_col):
        fac_copy(d).wait_recv()
        total = total + fac_recv[d].astype(F32)
    fac_all[me] = total.astype(BF)
    for d in range(1, n_row):
        all_copy(d).start()
    total = piece_send[me].astype(F32)
    for d in range(1, n_row):
        piece_copy(d).wait_recv()
        total = total + piece_recv[d].astype(F32)
    piece_all[me] = total.astype(BF)
    for d in range(1, n_row):
        gat_copy(d).start()

    for d in range(1, n_row):
        all_arrival(d).wait_recv()
    query_all, hidden_all = [], []
    for r in range(n_row):
        block = fac_all[r].astype(F32)
        block = jnp.concatenate([block[:, : 2 * rank], block[:, 2 * rank : 4 * rank]], axis=0)
        query_all.append(block[:, :rank].astype(BF))
        hidden_all.append((block[:, rank : 2 * rank] * sign_of(r * blk)).astype(BF))
    dq_ref[...] = SCALE * mm(jnp.concatenate(query_all, axis=0), x[...], 0, 0)
    du_ref[...] = SCALE * mm(jnp.concatenate(hidden_all, axis=0), cot[...], 0, 0)
    for d in range(1, n_row):
        gat_arrival(d).wait_recv()
    for r in range(n_row):
        pieces_ref[r * share : (r + 1) * share, :] = piece_all[r].astype(F32)

    for d in range(1, n_row):
        for c in range(2 * n_chunk):
            chunk_copy(c, d).wait_send()
        small_copy(d).wait_send()
        all_copy(d).wait_send()
        piece_copy(d).wait_send()
        gat_copy(d).wait_send()
    for d in range(1, n_col):
        fac_copy(d).wait_send()


def local(
    activations,
    cotangent,
    forget,
    lengths,
    query_weight,
    key_weight,
    value_weight,
    output_projection_weight,
    query_down,
    query_up,
    output_down,
    output_up,
):
    n_row, n_col = lax.axis_size("row"), lax.axis_size("col")
    tokens, depth = activations.shape
    cols = query_weight.shape[1]
    rank = query_down.shape[1]
    blk = tokens // n_row
    width = min(256, cols)
    n_chunk = cols // width
    share = 2 * rank // n_row
    any_spec = pl.BlockSpec(memory_space=pl.ANY)
    vmem = pl.BlockSpec(memory_space=pltpu.VMEM)
    dma = pltpu.SemaphoreType.DMA
    dq, pieces, du = pl.pallas_call(
        functools.partial(kernel, n_row, n_col),
        out_shape=(
            jax.ShapeDtypeStruct((rank, depth), F32),
            jax.ShapeDtypeStruct((2 * rank, cols), F32),
            jax.ShapeDtypeStruct((rank, depth), F32),
        ),
        in_specs=[pl.BlockSpec(memory_space=pltpu.SMEM), vmem] + [any_spec] * 10,
        out_specs=(vmem, vmem, vmem),
        scratch_shapes=[
            pltpu.VMEM((tokens, depth), BF),
            pltpu.VMEM((tokens, depth), BF),
            pltpu.VMEM((n_chunk, depth, width), BF),
            pltpu.VMEM((2, depth, HD), BF),
            pltpu.VMEM((n_chunk, width, depth), BF),
            pltpu.VMEM((depth, rank), BF),
            pltpu.VMEM((n_chunk, rank, width), BF),
            pltpu.VMEM((cols, rank), BF),
            pltpu.VMEM((rank, depth), BF),
            pltpu.VMEM((2, tokens, rank), BF),
            pltpu.VMEM((2 * n_chunk, n_row, blk, width), BF),
            pltpu.VMEM((2 * n_chunk, n_row, blk, width), BF),
            pltpu.VMEM((n_row, blk, 3 * HD), BF),
            pltpu.VMEM((n_row, blk, 3 * HD), BF),
            pltpu.VMEM((blk // 2, 4 * rank), BF),
            pltpu.VMEM((n_col, blk // 2, 4 * rank), BF),
            pltpu.VMEM((n_row, blk // 2, 4 * rank), BF),
            pltpu.VMEM((n_row, share, cols), BF),
            pltpu.VMEM((n_row, share, cols), BF),
            pltpu.VMEM((n_row, share, cols), BF),
            dma((7 + n_chunk,)),
            dma((n_chunk,)),
            dma((n_chunk,)),
            dma((2 * n_chunk, n_row)),
            dma((2 * n_chunk, n_row)),
            dma((n_row,)),
            dma((n_row,)),
            dma((n_col,)),
            dma((n_col,)),
            dma((n_row,)),
            dma((n_row,)),
            dma((n_row,)),
            dma((n_row,)),
            dma((n_row,)),
            dma((n_row,)),
        ],
        compiler_params=pltpu.CompilerParams(
            collective_id=0, has_side_effects=True, vmem_limit_bytes=50 << 20
        ),
        name="unlearn_step",
    )(
        lengths,
        forget.reshape(1, tokens),
        activations,
        cotangent,
        query_weight,
        key_weight,
        value_weight,
        output_projection_weight,
        query_down,
        query_up,
        output_down,
        output_up,
    )
    return dq.T, pieces[:rank], pieces[rank:].T, du


def solution(mesh):
    placed = (
        P(None, "row"),
        P(None, "row"),
        P(),
        P("row", None),
        P("row", "col"),
        P("row", None),
        P("row", None),
        P("col", "row"),
        P("row", None),
        P(None, "col"),
        P("col", None),
        P(None, "row"),
    )
    return jax.shard_map(
        local,
        mesh=mesh,
        in_specs=placed,
        out_specs=(P("row", None), P(None, "col"), P("col", None), P(None, "row")),
        check_vma=False,
    )
```

time: 181 us -> 40.8 us (0.23)
  waiting for transfers between devices: 85.3 us -> 0 us
  blocking collectives: 39.9 us -> 0 us
  matrix products: 33.5 us -> 0 us
  Pallas kernels: 0 us -> 32 us
  between operations: 14 us -> 0.66 us
  local copies, waits for them, and re-layouts: 2.51 us -> 7.86 us
  other arithmetic: 5.14 us -> 0 us
    reduce_scatter x2 -> x0, waiting for transfers between devices: 43.5 us -> none  [the longest x1 25.9 us: local(): lax.psum_scatter(jnp.concatenate([hidden_state_term, reduced_result], axi...]
    psum x1 -> x0, waiting for transfers between devices: 41.8 us -> none  [local(): lax.psum(up_projection_piece.astype(jnp.bfloat16), 'row')]
    psum x1 -> x0, blocking collectives: 39.9 us -> none  [local(): lax.psum((query_padded, hidden_padded), ('row', 'col'))]
    dot_general x17 -> x0, matrix products: 32.3 us -> none  [the longest x2 8.79 us: row_contraction(): lax.dot_general(left, right, (((1,), (1,)), ((), ())), preferred_element_...]
    pallas_call x0 -> x1, Pallas kernels: none -> 32 us  [local(): pl.pallas_call(functools.partial(kernel, n_row, n_col), out_shape=(jax.Sh...]
    unnamed x12, local copies, waits for them, and re-layouts: 1.56 us -> 7.14 us
    convert_element_type x3 -> x0, other arithmetic: 3.01 us -> none  [the longest x1 1.5 us: local(): lax.psum(up_projection_piece.astype(jnp.bfloat16), 'row')]
  transfers between devices with their start and end apart: 3 -> 0, of which waited for: 3 -> 0; matrix products, arithmetic and copies ran while one was open for 8% -> 0% of each run, Pallas kernels for 0% -> 0%
where the time goes in v1:
time: 40.8 us; the launch traced here: 40.5 us
  Pallas kernels  32 us (78%)
  local copies, waits for them, and re-layouts  7.86 us (19%)
  between operations  0.66 us (2%)
    pallas_call x1, Pallas kernels, local(): pl.pallas_call(functools.partial(kernel, n_row, n_col), out_shape=(jax.Sh...  32 us
    unnamed x12, local copies, waits for them, and re-layouts  7.14 us

profile of v1, /device:TPU:0, one launch (start us, length us, event | category | flops | bytes accessed | tf_op | source)
XLA Modules:
  0.0 40.5 jit_solution(12984283696785168518)
XLA Ops:
  0.6 1.0 %copy.17.od_hbm = bf16[1024,32]{1,0:T(8,128)(2,1)S(1)} copy(bf16[1024,32]{0,1:T(8,128)(2,1)} %param.22) | data formatting | bytes 131072 | tf_op args[10]
  1.6 1.4 %copy.16.qd_hbm = bf16[4096,32]{1,0:T(8,128)(2,1)S(1)} copy(bf16[4096,32]{0,1:T(8,128)(2,1)} %param.20) | data formatting | bytes 524288 | tf_op args[8]
  3.1 0.0 copy-start
  3.1 0.9 %copy-done = bf16[32,4096]{1,0:T(8,128)(2,1)S(1)} copy-done((bf16[32,4096]{1,0:T(8,128)(2,1)S(1)}, bf16[32,4096]{1,0:T(8,128)(2,1)}, u32[]{:S(2)}) %copy-start) | copy-done | bytes 262168
  4.0 0.0 copy-start.1
  4.0 0.8 %copy-done.1 = bf16[32,1024]{1,0:T(8,128)(2,1)S(1)} copy-done((bf16[32,1024]{1,0:T(8,128)(2,1)S(1)}, bf16[32,1024]{1,0:T(8,128)(2,1)}, u32[]{:S(2)}) %copy-start.1) | copy-done | bytes 65560
  4.9 0.0 copy-start.2
  4.9 0.7 %copy-done.2 = s32[256]{0:T(256)S(1)} copy-done((s32[256]{0:T(256)S(1)}, s32[256]{0:T(256)}, u32[]{:S(2)}) %copy-start.2) | copy-done | bytes 1048
  5.6 0.0 copy-start.3
  5.6 0.7 %copy-done.3 = s32[1,4]{1,0:T(1,128)S(1)} copy-done((s32[1,4]{1,0:T(1,128)S(1)}, s32[1,4]{1,0:T(1,128)}, u32[]{:S(2)}) %copy-start.3) | copy-done | bytes 40
  6.2 32.0 %unlearn_step.1 = (f32[32,4096]{1,0:T(8,128)S(1)}, f32[64,1024]{1,0:T(8,128)S(1)}, f32[32,4096]{1,0:T(8,128)S(1)}) custom-call(s32[1,4]{1,0:T(1,128)S(1)} %copy-done.3, s32[1,256]{1,0:T(1,128)S(1)} %bitcast.5, bf16[256,4096]{1,0:T(8,128)(2,1)} %x_hbm.1, bf16[256,4096]{1,0:T(8,128)(2,1)} %cot_hbm.1, bf16[4096,1024]{1,0:T(8,128)(2,1)} %wq_hbm.1, ...), custom_call_target="tpu_custom_call" | custom-call | tf_op jit(solution)/shard_map/unlearn_step/pallas_call | solution.py:378
  38.2 0.7 %slice_bitcast_fusion = (f32[1024,32]{0,1:T(8,128)}, f32[32,1024]{1,0:T(8,128)}) fusion(f32[64,1024]{1,0:T(8,128)S(1)} %get-tuple-element.8), kind=kLoop, calls=%fused_computation | loop fusion | bytes 524288 | tf_op jit(solution)/shard_map/transpose | solution.py:442
  38.9 0.8 %copy.20 = f32[4096,32]{0,1:T(8,128)} copy(f32[4096,32]{0,1:T(8,128)S(1)} %bitcast.4) | data formatting | bytes 1048576
  39.7 0.8 %copy.21 = f32[32,4096]{1,0:T(8,128)} copy(f32[32,4096]{1,0:T(8,128)S(1)} %get-tuple-element.19) | data formatting | bytes 1048576
Async XLA Ops:
  3.1 1.0 %copy-start = (bf16[32,4096]{1,0:T(8,128)(2,1)S(1)}, bf16[32,4096]{1,0:T(8,128)(2,1)}, u32[]{:S(2)}) copy-start(bf16[32,4096]{1,0:T(8,128)(2,1)} %ou_hbm.1) | copy-start | bytes 786436
  4.0 0.8 %copy-start.1 = (bf16[32,1024]{1,0:T(8,128)(2,1)S(1)}, bf16[32,1024]{1,0:T(8,128)(2,1)}, u32[]{:S(2)}) copy-start(bf16[32,1024]{1,0:T(8,128)(2,1)} %up_hbm.1) | copy-start | bytes 196612
  4.9 0.7 %copy-start.2 = (s32[256]{0:T(256)S(1)}, s32[256]{0:T(256)}, u32[]{:S(2)}) copy-start(s32[256]{0:T(256)} %param.14) | copy-start | bytes 3076
  5.6 0.7 %copy-start.3 = (s32[1,4]{1,0:T(1,128)S(1)}, s32[1,4]{1,0:T(1,128)}, u32[]{:S(2)}) copy-start(s32[1,4]{1,0:T(1,128)} %lengths_ref.1) | copy-start | bytes 52

commit v2 on v1

--- a/solution.py
+++ b/solution.py
@@ -26,8 +26,8 @@
 def kernel(
     n_row,
     n_col,
-    lengths_ref,
-    forget_ref,
+    lengths_hbm,
+    forget_hbm,
     x_hbm,
     cot_hbm,
     wq_hbm,
@@ -61,6 +61,8 @@
     piece_send,
     piece_recv,
     piece_all,
+    lengths_ref,
+    forget_ref,
     load_sem,
     wq_sem,
     wo_sem,
@@ -80,7 +82,7 @@
     me = lax.axis_index("row")
     mc = lax.axis_index("col")
     n_chunk, depth, width = wq.shape
-    rank = qd.shape[1]
+    rank = qd.shape[0]
     tokens = x.shape[0]
     blk = tokens // n_row
     heads = n_chunk * width // HD
@@ -107,7 +109,12 @@
 
     def up_load(c):
         return pltpu.make_async_copy(
-            up_hbm.at[:, pl.ds(c * width, width)], up.at[c], load_sem.at[7 + c]
+            up_hbm.at[:, pl.ds(c * width, width)], up.at[c], load_sem.at[8 + c]
+        )
+
+    def od_load(c):
+        return pltpu.make_async_copy(
+            od_hbm.at[:, pl.ds(c * width, width)], od.at[c], load_sem.at[8 + n_chunk + c]
         )
 
     load_x = pltpu.make_async_copy(x_hbm, x, load_sem.at[0])
@@ -116,7 +123,8 @@
     load_v = pltpu.make_async_copy(wv_hbm.at[:, group_cols], wkv.at[1], load_sem.at[3])
     load_cot = pltpu.make_async_copy(cot_hbm, cot, load_sem.at[4])
     load_ou = pltpu.make_async_copy(ou_hbm, ou, load_sem.at[5])
-    load_od = pltpu.make_async_copy(od_hbm, od, load_sem.at[6])
+    load_len = pltpu.make_async_copy(lengths_hbm, lengths_ref, load_sem.at[6])
+    load_forget = pltpu.make_async_copy(forget_hbm, forget_ref, load_sem.at[7])
     load_x.start()
     load_qd.start()
     for c in range(n_chunk):
@@ -127,7 +135,10 @@
     load_v.start()
     load_cot.start()
     load_ou.start()
-    load_od.start()
+    for c in range(n_chunk):
+        od_load(c).start()
+    load_len.start()
+    load_forget.start()
     for c in range(n_chunk):
         load_wo(c).start()
 
@@ -161,38 +172,85 @@
         p = row_peer(d)
         return remote(small_send.at[p], small_recv.at[d], small_ss.at[d], small_rs.at[d], {"row": p})
 
-    def fac_copy(d):
-        return remote(fac_send, fac_recv.at[d], fac_ss.at[d], fac_rs.at[d], {"col": col_peer(d)})
-
-    def all_copy(d):
+    def fac_copy(j, d):
         return remote(
-            fac_all.at[me], fac_all.at[me], all_ss.at[d], all_rs.at[d], {"row": row_peer(d)}
-        )
-
-    def all_arrival(d):
+            fac_send.at[j], fac_recv.at[j, d], fac_ss.at[j, d], fac_rs.at[j, d], {"col": col_peer(d)}
+        )
+
+    def all_copy(j, d, owner):
         return remote(
-            fac_all.at[me], fac_all.at[row_peer(n_row - d)], all_ss.at[d], all_rs.at[d], {"row": row_peer(d)}
-        )
-
-    def piece_copy(d):
+            fac_all.at[j, me], fac_all.at[j, owner], all_ss.at[j, d], all_rs.at[j, d], {"row": row_peer(d)}
+        )
+
+    def piece_copy(j, d):
         p = row_peer(d)
-        return remote(piece_send.at[p], piece_recv.at[d], piece_ss.at[d], piece_rs.at[d], {"row": p})
-
-    def gat_copy(d):
         return remote(
-            piece_all.at[me], piece_all.at[me], gat_ss.at[d], gat_rs.at[d], {"row": row_peer(d)}
-        )
-
-    def gat_arrival(d):
+            piece_send.at[j, p], piece_recv.at[j, d], piece_ss.at[j, d], piece_rs.at[j, d], {"row": p}
+        )
+
+    def gat_copy(j, d, owner):
         return remote(
-            piece_all.at[me], piece_all.at[row_peer(n_row - d)], gat_ss.at[d], gat_rs.at[d], {"row": row_peer(d)}
-        )
+            piece_all.at[j, me], piece_all.at[j, owner], gat_ss.at[j, d], gat_rs.at[j, d], {"row": row_peer(d)}
+        )
+
+    quarter = blk // 4
+    share = piece_send.shape[2]
+
+    def send_factor(j, factor):
+        packed = jnp.concatenate(
+            [factor[i * quarter : (i + 1) * quarter] for i in range(4)], axis=1
+        )
+        fac_send[j] = packed.astype(BF)
+        for d in range(1, n_col):
+            fac_copy(j, d).start()
+
+    def spread_factor(j):
+        total = fac_send[j].astype(F32)
+        for d in range(1, n_col):
+            fac_copy(j, d).wait_recv()
+            total = total + fac_recv[j, d].astype(F32)
+        fac_all[j, me] = total.astype(BF)
+        for d in range(1, n_row):
+            all_copy(j, d, me).start()
+
+    def factor_everywhere(j):
+        for d in range(1, n_row):
+            all_copy(j, d, row_peer(n_row - d)).wait_recv()
+        blocks = []
+        for r in range(n_row):
+            block = fac_all[j, r].astype(F32)
+            blocks.append(
+                jnp.concatenate([block[:, i * rank : (i + 1) * rank] for i in range(4)], axis=0)
+            )
+        return blocks
+
+    def send_piece(j, piece):
+        for r in range(n_row):
+            piece_send[j, r] = piece[r * share : (r + 1) * share].astype(BF)
+        for d in range(1, n_row):
+            piece_copy(j, d).start()
+
+    def spread_piece(j):
+        total = piece_send[j, me].astype(F32)
+        for d in range(1, n_row):
+            piece_copy(j, d).wait_recv()
+            total = total + piece_recv[j, d].astype(F32)
+        piece_all[j, me] = total.astype(BF)
+        for d in range(1, n_row):
+            gat_copy(j, d, me).start()
+
+    def finish_piece(j):
+        for d in range(1, n_row):
+            gat_copy(j, d, row_peer(n_row - d)).wait_recv()
+        for r in range(n_row):
+            first = j * rank + r * share
+            pieces_ref[first : first + share, :] = piece_all[j, r].astype(F32)
 
     load_x.wait()
     load_qd.wait()
     for c in range(n_chunk):
         up_load(c).wait()
-    lowrank = mm(x[...], qd[...], 1, 0)
+    lowrank = mm(x[...], qd[...], 1, 1)
     red[0] = lowrank.astype(BF)
     pl.semaphore_wait(barrier, n_row + n_col - 2)
 
@@ -212,7 +270,8 @@
     small_send[:, :, HD : 2 * HD] = mm(x[...], wkv[1], 1, 0).astype(BF).reshape(n_row, blk, HD)
     load_cot.wait()
     load_ou.wait()
-    load_od.wait()
+    for c in range(n_chunk):
+        od_load(c).wait()
     red[1] = mm(cot[...], ou[...], 1, 1).astype(BF)
     small_send[:, :, 2 * HD :] = jnp.concatenate(
         [red[0], red[1], jnp.zeros((tokens, HD - 2 * rank), BF)], axis=1
@@ -225,8 +284,7 @@
         pltpu.make_async_copy(
             wo_hbm.at[pl.ds(0, width), :], wo.at[c], wo_sem.at[c]
         ).wait()
-        down = od[pl.ds(pl.multiple_of(c * width, width), width), :]
-        term = mm(cot[...], wo[c], 1, 1) + SCALE * mm(red[1], down, 1, 1)
+        term = mm(cot[...], wo[c], 1, 1) + SCALE * mm(red[1], od[c], 1, 0)
         chunk_send[n_chunk + c] = term.astype(BF).reshape(n_row, blk, width)
         for d in range(1, n_row):
             chunk_copy(n_chunk + c, d).start()
@@ -244,6 +302,8 @@
         picked = jnp.where(lane == sub + first, forget_ref[...], 0)
         return (1 - 2 * jnp.sum(picked, axis=1, keepdims=True)).astype(F32)
 
+    load_len.wait()
+    load_forget.wait()
     sign = sign_of(me * blk)
 
     stacked = []
@@ -277,77 +337,65 @@
     softmax = numer / jnp.sum(numer, axis=1, keepdims=True)
     hidden = mm(softmax.astype(BF), value, 1, 0).astype(BF)
     hidden_flat = jnp.concatenate([hidden[h * blk : (h + 1) * blk] for h in range(heads)], axis=1)
-    hidden_factor = mm(hidden_flat, od[...], 1, 0)
-    down_piece = SCALE * mm(grad_low, hidden_flat, 0, 0)
-
-    stacked = []
+    hidden_factor = mm(hidden_flat[:, 0:width], od[0], 1, 1)
+    for c in range(1, n_chunk):
+        hidden_factor = hidden_factor + mm(hidden_flat[:, c * width : (c + 1) * width], od[c], 1, 1)
+    send_factor(1, hidden_factor)
+    send_piece(1, SCALE * mm(grad_low, hidden_flat, 0, 0))
+    signs = [sign_of(r * blk) for r in range(n_row)]
+    spread_factor(1)
+
+    query_factor = jnp.zeros((blk, rank), F32)
+    up_parts = []
+    span = per * blk
     for c in range(n_chunk):
         part = (chunk_sum(n_chunk + c) * sign).astype(BF)
-        for h in range(per):
-            stacked.append(part[:, h * HD : (h + 1) * HD])
-    hidden_grad = jnp.concatenate(stacked, axis=0)
-    prob_grad = mm(hidden_grad, value, 1, 1)
-    score_grad = softmax * (prob_grad - jnp.sum(prob_grad * softmax, axis=1, keepdims=True))
-    query_grad = (mm(score_grad.astype(BF), key, 1, 0) * inverse).astype(BF)
-    grad_flat = jnp.concatenate(
-        [query_grad[h * blk : (h + 1) * blk] for h in range(heads)], axis=1
-    )
-    query_factor = mm(grad_flat[:, 0:width], up[0], 1, 1)
-    for c in range(1, n_chunk):
-        query_factor = query_factor + mm(grad_flat[:, c * width : (c + 1) * width], up[c], 1, 1)
-    factors = jnp.concatenate([query_factor, hidden_factor], axis=1)
-    half = blk // 2
-    packed = jnp.concatenate([factors[:half], factors[half:]], axis=1)
-    fac_send[...] = packed.astype(BF)
-    for d in range(1, n_col):
-        fac_copy(d).start()
-    up_piece = SCALE * mm(in_low, grad_flat, 0, 0)
-    both = jnp.concatenate([up_piece, down_piece], axis=0).astype(BF)
-    share = piece_send.shape[1]
-    for r in range(n_row):
-        piece_send[r] = both[r * share : (r + 1) * share]
-    for d in range(1, n_row):
-        piece_copy(d).start()
-
-    total = fac_send[...].astype(F32)
-    for d in range(1, n_col):
-        fac_copy(d).wait_recv()
-        total = total + fac_recv[d].astype(F32)
-    fac_all[me] = total.astype(BF)
-    for d in range(1, n_row):
-        all_copy(d).start()
-    total = piece_send[me].astype(F32)
-    for d in range(1, n_row):
-        piece_copy(d).wait_recv()
-        total = total + piece_recv[d].astype(F32)
-    piece_all[me] = total.astype(BF)
-    for d in range(1, n_row):
-        gat_copy(d).start()
-
-    for d in range(1, n_row):
-        all_arrival(d).wait_recv()
-    query_all, hidden_all = [], []
-    for r in range(n_row):
-        block = fac_all[r].astype(F32)
-        block = jnp.concatenate([block[:, : 2 * rank], block[:, 2 * rank : 4 * rank]], axis=0)
-        query_all.append(block[:, :rank].astype(BF))
-        hidden_all.append((block[:, rank : 2 * rank] * sign_of(r * blk)).astype(BF))
-    dq_ref[...] = SCALE * mm(jnp.concatenate(query_all, axis=0), x[...], 0, 0)
-    du_ref[...] = SCALE * mm(jnp.concatenate(hidden_all, axis=0), cot[...], 0, 0)
-    for d in range(1, n_row):
-        gat_arrival(d).wait_recv()
-    for r in range(n_row):
-        pieces_ref[r * share : (r + 1) * share, :] = piece_all[r].astype(F32)
+        hidden_grad = jnp.concatenate([part[:, h * HD : (h + 1) * HD] for h in range(per)], axis=0)
+        soft = softmax[c * span : (c + 1) * span]
+        prob_grad = mm(hidden_grad, value, 1, 1)
+        score_grad = soft * (prob_grad - jnp.sum(prob_grad * soft, axis=1, keepdims=True))
+        query_grad = (mm(score_grad.astype(BF), key, 1, 0) * inverse).astype(BF)
+        flat = jnp.concatenate([query_grad[h * blk : (h + 1) * blk] for h in range(per)], axis=1)
+        query_factor = query_factor + mm(flat, up[c], 1, 1)
+        up_parts.append(SCALE * mm(in_low, flat, 0, 0))
+    send_factor(0, query_factor)
+    send_piece(0, jnp.concatenate(up_parts, axis=1))
+
+    spread_piece(1)
+    blocks = [(b * s).astype(BF) for b, s in zip(factor_everywhere(1), signs)]
+    du_ref[...] = SCALE * mm(jnp.concatenate(blocks, axis=0), cot[...], 0, 0)
+    spread_factor(0)
+    spread_piece(0)
+    blocks = [b.astype(BF) for b in factor_everywhere(0)]
+    dq_ref[...] = SCALE * mm(jnp.concatenate(blocks, axis=0), x[...], 0, 0)
+    finish_piece(1)
+    finish_piece(0)
 
     for d in range(1, n_row):
         for c in range(2 * n_chunk):
             chunk_copy(c, d).wait_send()
         small_copy(d).wait_send()
-        all_copy(d).wait_send()
-        piece_copy(d).wait_send()
-        gat_copy(d).wait_send()
+        for j in range(2):
+            all_copy(j, d, me).wait_send()
+            piece_copy(j, d).wait_send()
+            gat_copy(j, d, me).wait_send()
     for d in range(1, n_col):
-        fac_copy(d).wait_send()
+        for j in range(2):
+            fac_copy(j, d).wait_send()
+
+
+def writer(dq, pieces, du, o_qd, o_up, o_od, o_ou, sem):
+    rank = dq.shape[0]
+    moves = [
+        pltpu.make_async_copy(dq, o_qd, sem.at[0]),
+        pltpu.make_async_copy(du, o_ou, sem.at[1]),
+        pltpu.make_async_copy(pieces.at[pl.ds(0, rank)], o_up, sem.at[2]),
+        pltpu.make_async_copy(pieces.at[pl.ds(rank, rank)], o_od, sem.at[3]),
+    ]
+    for move in moves:
+        move.start()
+    for move in moves:
+        move.wait()
 
 
 def local(
@@ -371,8 +419,8 @@
     blk = tokens // n_row
     width = min(256, cols)
     n_chunk = cols // width
-    share = 2 * rank // n_row
-    any_spec = pl.BlockSpec(memory_space=pl.ANY)
+    share = rank // n_row
+    hbm = pl.BlockSpec(memory_space=pltpu.HBM)
     vmem = pl.BlockSpec(memory_space=pltpu.VMEM)
     dma = pltpu.SemaphoreType.DMA
     dq, pieces, du = pl.pallas_call(
@@ -382,7 +430,7 @@
             jax.ShapeDtypeStruct((2 * rank, cols), F32),
             jax.ShapeDtypeStruct((rank, depth), F32),
         ),
-        in_specs=[pl.BlockSpec(memory_space=pltpu.SMEM), vmem] + [any_spec] * 10,
+        in_specs=[hbm] * 12,
         out_specs=(vmem, vmem, vmem),
         scratch_shapes=[
             pltpu.VMEM((tokens, depth), BF),
@@ -390,56 +438,77 @@
             pltpu.VMEM((n_chunk, depth, width), BF),
             pltpu.VMEM((2, depth, HD), BF),
             pltpu.VMEM((n_chunk, width, depth), BF),
-            pltpu.VMEM((depth, rank), BF),
+            pltpu.VMEM((rank, depth), BF),
             pltpu.VMEM((n_chunk, rank, width), BF),
-            pltpu.VMEM((cols, rank), BF),
+            pltpu.VMEM((n_chunk, rank, width), BF),
             pltpu.VMEM((rank, depth), BF),
             pltpu.VMEM((2, tokens, rank), BF),
             pltpu.VMEM((2 * n_chunk, n_row, blk, width), BF),
             pltpu.VMEM((2 * n_chunk, n_row, blk, width), BF),
             pltpu.VMEM((n_row, blk, 3 * HD), BF),
             pltpu.VMEM((n_row, blk, 3 * HD), BF),
-            pltpu.VMEM((blk // 2, 4 * rank), BF),
-            pltpu.VMEM((n_col, blk // 2, 4 * rank), BF),
-            pltpu.VMEM((n_row, blk // 2, 4 * rank), BF),
-            pltpu.VMEM((n_row, share, cols), BF),
-            pltpu.VMEM((n_row, share, cols), BF),
-            pltpu.VMEM((n_row, share, cols), BF),
-            dma((7 + n_chunk,)),
+            pltpu.VMEM((2, blk // 4, 4 * rank), BF),
+            pltpu.VMEM((2, n_col, blk // 4, 4 * rank), BF),
+            pltpu.VMEM((2, n_row, blk // 4, 4 * rank), BF),
+            pltpu.VMEM((2, n_row, share, cols), BF),
+            pltpu.VMEM((2, n_row, share, cols), BF),
+            pltpu.VMEM((2, n_row, share, cols), BF),
+            pltpu.SMEM(lengths.shape, jnp.int32),
+            pltpu.VMEM((1, tokens), jnp.int32),
+            dma((8 + 2 * n_chunk,)),
             dma((n_chunk,)),
             dma((n_chunk,)),
             dma((2 * n_chunk, n_row)),
             dma((2 * n_chunk, n_row)),
             dma((n_row,)),
             dma((n_row,)),
-            dma((n_col,)),
-            dma((n_col,)),
-            dma((n_row,)),
-            dma((n_row,)),
-            dma((n_row,)),
-            dma((n_row,)),
-            dma((n_row,)),
-            dma((n_row,)),
+            dma((2, n_col)),
+            dma((2, n_col)),
+            dma((2, n_row)),
+            dma((2, n_row)),
+            dma((2, n_row)),
+            dma((2, n_row)),
+            dma((2, n_row)),
+            dma((2, n_row)),
         ],
         compiler_params=pltpu.CompilerParams(
             collective_id=0, has_side_effects=True, vmem_limit_bytes=50 << 20
         ),
         name="unlearn_step",
     )(
-        lengths,
-        forget.reshape(1, tokens),
-        activations,
-        cotangent,
-        query_weight,
-        key_weight,
-        value_weight,
-        output_projection_weight,
-        query_down,
-        query_up,
-        output_down,
-        output_up,
+        *(
+            pltpu.with_memory_space_constraint(operand, pltpu.HBM)
+            for operand in (
+                lengths,
+                forget.reshape(1, tokens),
+                activations,
+                cotangent,
+                query_weight,
+                key_weight,
+                value_weight,
+                output_projection_weight,
+                query_down.T,
+                query_up,
+                output_down.T,
+                output_up,
+            )
+        )
     )
-    return dq.T, pieces[:rank], pieces[rank:].T, du
+    down_grad, up_grad, out_down_grad, out_up_grad = pl.pallas_call(
+        writer,
+        out_shape=(
+            jax.ShapeDtypeStruct((rank, depth), F32),
+            jax.ShapeDtypeStruct((rank, cols), F32),
+            jax.ShapeDtypeStruct((rank, cols), F32),
+            jax.ShapeDtypeStruct((rank, depth), F32),
+        ),
+        in_specs=[pl.BlockSpec(memory_space=pl.ANY)] * 3,
+        out_specs=(hbm,) * 4,
+        scratch_shapes=[dma((4,))],
+        compiler_params=pltpu.CompilerParams(vmem_limit_bytes=1 << 20),
+        name="write_outputs",
+    )(dq, pieces, du)
+    return down_grad.T, up_grad, out_down_grad.T, out_up_grad
 
 
 def solution(mesh):

time: 40.8 us -> 36.2 us (0.89)
  local copies, waits for them, and re-layouts: 7.86 us -> 0 us
  Pallas kernels: 32 us -> 35.5 us
    unnamed x12 -> x0, local copies, waits for them, and re-layouts: 7.14 us -> none
    pallas_call x1, Pallas kernels: 32 us -> 34.4 us  [local(): pl.pallas_call(functools.partial(kernel, n_row, n_col), out_shape=(jax.Sh...]
    pallas_call x0 -> x1, Pallas kernels: none -> 1.08 us  [local(): pl.pallas_call(writer, out_shape=(jax.ShapeDtypeStruct((rank, depth), F32...]
    transpose x1 -> x0, local copies, waits for them, and re-layouts: 0.72 us -> none  [local(): return (dq.T, pieces[:rank], pieces[rank:].T, du)]
where the time goes in v2:
time: 36.2 us; the launch traced here: 36.1 us
  Pallas kernels  35.5 us (98%)
  between operations  0.64 us (2%)
    pallas_call x1, Pallas kernels, local(): pl.pallas_call(functools.partial(kernel, n_row, n_col), out_shape=(jax.Sh...  34.4 us
    pallas_call x1, Pallas kernels, local(): pl.pallas_call(writer, out_shape=(jax.ShapeDtypeStruct((rank, depth), F32...  1.08 us

profile of v2, /device:TPU:0, one launch (start us, length us, event | category | flops | bytes accessed | tf_op | source)
XLA Modules:
  0.0 36.1 jit_solution(16148984415945212948)
XLA Ops:
  0.6 34.4 %unlearn_step.1 = (f32[32,4096]{1,0:T(8,128)S(1)}, f32[64,1024]{1,0:T(8,128)S(1)}, f32[32,4096]{1,0:T(8,128)S(1)}) custom-call(s32[1,4]{1,0:T(1,128)} %lengths_hbm.1, s32[1,256]{1,0:T(1,128)} %bitcast.7, bf16[256,4096]{1,0:T(8,128)(2,1)} %x_hbm.1, bf16[256,4096]{1,0:T(8,128)(2,1)} %cot_hbm.1, bf16[4096,1024]{1,0:T(8,128)(2,1)} %wq_hbm.1, ...), custom_call_target="tpu_custom_call" | custom-call | tf_op jit(solution)/shard_map/unlearn_step/pallas_call | solution.py:426
  35.0 1.1 %write_outputs.1 = (f32[32,4096]{1,0:T(8,128)}, f32[32,1024]{1,0:T(8,128)}, f32[32,1024]{1,0:T(8,128)}, f32[32,4096]{1,0:T(8,128)}) custom-call(f32[32,4096]{1,0:T(8,128)S(1)} %get-tuple-element.11.dq, f32[64,1024]{1,0:T(8,128)S(1)} %get-tuple-element.12.pieces, f32[32,4096]{1,0:T(8,128)S(1)} %get-tuple-element.13.du), custom_call_target="tpu_custom_call" | custom-call | tf_op jit(solution)/shard_map/write_outputs/pallas_call | solution.py:497

commit v3 on v2

--- a/solution.py
+++ b/solution.py
@@ -343,7 +343,6 @@
     send_factor(1, hidden_factor)
     send_piece(1, SCALE * mm(grad_low, hidden_flat, 0, 0))
     signs = [sign_of(r * blk) for r in range(n_row)]
-    spread_factor(1)
 
     query_factor = jnp.zeros((blk, rank), F32)
     up_parts = []
@@ -361,11 +360,12 @@
     send_factor(0, query_factor)
     send_piece(0, jnp.concatenate(up_parts, axis=1))
 
+    spread_factor(1)
+    spread_factor(0)
     spread_piece(1)
+    spread_piece(0)
     blocks = [(b * s).astype(BF) for b, s in zip(factor_everywhere(1), signs)]
     du_ref[...] = SCALE * mm(jnp.concatenate(blocks, axis=0), cot[...], 0, 0)
-    spread_factor(0)
-    spread_piece(0)
     blocks = [b.astype(BF) for b in factor_everywhere(0)]
     dq_ref[...] = SCALE * mm(jnp.concatenate(blocks, axis=0), x[...], 0, 0)
     finish_piece(1)

time: 36.2 us -> 36.3 us (level)
  no operation moved by 1% of the time
where the time goes in v3:
time: 36.3 us; the launch traced here: 36.1 us
  Pallas kernels  35.5 us (98%)
  between operations  0.64 us (2%)
    pallas_call x1, Pallas kernels, local(): pl.pallas_call(functools.partial(kernel, n_row, n_col), out_shape=(jax.Sh...  34.4 us
    pallas_call x1, Pallas kernels, local(): pl.pallas_call(writer, out_shape=(jax.ShapeDtypeStruct((rank, depth), F32...  1.08 us

profile of v3, /device:TPU:0, one launch (start us, length us, event | category | flops | bytes accessed | tf_op | source)
XLA Modules:
  0.0 36.1 jit_solution(9205481897848946386)
XLA Ops:
  0.6 34.4 %unlearn_step.1 = (f32[32,4096]{1,0:T(8,128)S(1)}, f32[64,1024]{1,0:T(8,128)S(1)}, f32[32,4096]{1,0:T(8,128)S(1)}) custom-call(s32[1,4]{1,0:T(1,128)} %lengths_hbm.1, s32[1,256]{1,0:T(1,128)} %bitcast.7, bf16[256,4096]{1,0:T(8,128)(2,1)} %x_hbm.1, bf16[256,4096]{1,0:T(8,128)(2,1)} %cot_hbm.1, bf16[4096,1024]{1,0:T(8,128)(2,1)} %wq_hbm.1, ...), custom_call_target="tpu_custom_call" | custom-call | tf_op jit(solution)/shard_map/unlearn_step/pallas_call | solution.py:426
  35.0 1.1 %write_outputs.1 = (f32[32,4096]{1,0:T(8,128)}, f32[32,1024]{1,0:T(8,128)}, f32[32,1024]{1,0:T(8,128)}, f32[32,4096]{1,0:T(8,128)}) custom-call(f32[32,4096]{1,0:T(8,128)S(1)} %get-tuple-element.11.dq, f32[64,1024]{1,0:T(8,128)S(1)} %get-tuple-element.12.pieces, f32[32,4096]{1,0:T(8,128)S(1)} %get-tuple-element.13.du), custom_call_target="tpu_custom_call" | custom-call | tf_op jit(solution)/shard_map/write_outputs/pallas_call | solution.py:497
